TPU v7x, 32 devices: a whole 2x2x4 slice. The times are simulated.
32 devices in a mesh: ob: 8 (over z, core), pt: 4 (over y, x).
Axes of the slice: x: 2, y: 2, z: 4, core: 2. Of those that a mesh axis runs over, the one named last changes fastest.
Arguments:
- orbitals: float32 [128, 262144], P(('ob', 'pt')), may hold values from -32 to 32, as said below
- potential: float32 [262144], replicated, may hold values from 0 to 2
- cutoff: float32 [1], replicated, may hold values from 0.4 to 1
- eigvec: float32 [128, 128], replicated, may hold values from -3 to 3, as said below
Outputs:
- gram: float32 [128, 128], P(('ob', 'pt'))
- hamil_sub: float32 [128, 128], P(('ob', 'pt'))
- rotated: float32 [128, 262144], P(None, ('ob', 'pt'))
- residual: float32 [128, 262144], P(None, ('ob', 'pt'))
- ritz: float32 [128], replicated
Inputs may be any that keep to these rules, and one draw needn't show every extreme that they name: `orbitals`: each orbital is a rough field whose scale differs from orbital to orbital and from region to region of the grid. `eigvec`: A full-rank matrix with a unit-sized diagonal and independent off-diagonal entries.
All inputs are finite; a program needn't handle non-finite values.
Results may differ from a plain program's by a relative error of at most 0.00027.
Values sent between devices are 32-bit elements; how exact they have to be, the bound alone decides.
A program may use at most 128 MiB of HBM per device.

v0:
```python
import jax
import jax.numpy as jnp
from jax import lax
from jax.sharding import PartitionSpec as P

G = 64
DEGREE = 12
NPTS = 262144


upper_bound = 8.0
quot_eps = 1e-06


def apply_ham(fields, potential):
    points = fields.shape[-1]
    plane_len = G * G
    x_pair = jnp.roll(fields, plane_len, axis=-1) + jnp.roll(fields, -plane_len, axis=-1)
    cube_view = fields.reshape(fields.shape[0], G, plane_len)
    y_pair = (jnp.roll(cube_view, G, axis=-1) + jnp.roll(cube_view, -G, axis=-1)).reshape(
        fields.shape
    )
    z_index = lax.broadcasted_iota(jnp.int32, (1, points), 1) % G
    z_lower = jnp.where(
        z_index == 0, jnp.roll(fields, 1 - G, axis=-1), jnp.roll(fields, 1, axis=-1)
    )
    z_upper = jnp.where(
        z_index == G - 1, jnp.roll(fields, G - 1, axis=-1), jnp.roll(fields, -1, axis=-1)
    )
    return -0.5 * (x_pair + y_pair + z_lower + z_upper - 6.0 * fields) + potential * fields


def chebyshev(fields, potential, cutoff):
    center = 0.5 * (upper_bound + cutoff[0])
    half_width = 0.5 * (upper_bound - cutoff[0])
    current = (apply_ham(fields, potential) - center * fields) / half_width

    def advance(turn_idx, carry):
        previous, present = carry
        following = 2.0 * (apply_ham(present, potential) - center * present) / half_width - previous
        return (present, following)

    previous, current = lax.fori_loop(0, DEGREE - 1, advance, (fields, current))
    return (current, apply_ham(current, potential))


def on_device(orbitals, potential, cutoff, eigvec):
    high = lax.Precision.HIGHEST
    filtered, applied = chebyshev(orbitals, potential, cutoff)
    total_orb = eigvec.shape[0]
    n_ob = lax.axis_size("ob")
    n_pt = lax.axis_size("pt")
    per_dev = total_orb // (n_ob * n_pt)
    rows_filt, rows_appl = (
        lax.all_to_all(filtered, ("ob", "pt"), split_axis=1, concat_axis=0, tiled=True),
        lax.all_to_all(applied, ("ob", "pt"), split_axis=1, concat_axis=0, tiled=True),
    )
    part_gram = jnp.dot(rows_filt, rows_filt.T, precision=high) / NPTS
    part_hamil = jnp.dot(rows_filt, rows_appl.T, precision=high) / NPTS
    gram, hamil_sub = (
        lax.psum_scatter(part_gram, ("ob", "pt"), scatter_dimension=0, tiled=True),
        lax.psum_scatter(part_hamil, ("ob", "pt"), scatter_dimension=0, tiled=True),
    )
    rotated = jnp.dot(eigvec.T, rows_filt, precision=high)
    rot_applied = jnp.dot(eigvec.T, rows_appl, precision=high)
    my_index = lax.axis_index(("ob", "pt"))
    my_rows = lax.dynamic_slice_in_dim(eigvec, my_index * per_dev, per_dev, 0)
    numer = jnp.sum(my_rows * jnp.dot(hamil_sub, eigvec, precision=high), axis=0)
    denom = jnp.sum(my_rows * jnp.dot(gram, eigvec, precision=high), axis=0)
    numer, denom = lax.psum((numer, denom), ("ob", "pt"))
    ritz = numer / (denom + quot_eps)
    residual = rot_applied - ritz[:, None] * rotated
    return (gram, hamil_sub, rotated, residual, ritz)


def solution(mesh):
    return jax.shard_map(
        on_device,
        mesh=mesh,
        in_specs=(P(("ob", "pt"), None), P(), P(), P()),
        out_specs=(
            P(("ob", "pt"), None),
            P(("ob", "pt"), None),
            P(None, ("ob", "pt")),
            P(None, ("ob", "pt")),
            P(),
        ),
        check_vma=False,
    )
```

profile of v0, /device:TPU:0, one launch (start us, length us, event | category | flops | bytes accessed | tf_op | source)
XLA Modules:
  0.0 1040.0 jit_solution(13240792252912524412)
XLA Ops:
  13.5 4.6 fusion.57
  28.6 4.7 copy.22
  33.3 24.7 %fusion.29 = f32[4,262144]{1,0:T(4,128)} fusion(f32[4,262144]{1,0:T(4,128)} %copy-done.2, f32[4,1]{1,0:T(4,128)S(1)} %get-tuple-element.162, f32[4,262143]{1,0:T(4,128)} %get-tuple-element.164, f32[4,262081]{1,0:T(4,128)} %get-tuple-element.158, f32[4,63]{1,0:T(4,128)S(1)} %get-tuple-element.160, f32[4,262143]{1,0:T(4,128)} %get-tuple-element.163, ...), kind=kLoop, calls=%fused_computation.49 | loop fusion | flops 20971520 | bytes 39321608 | tf_op jit(solution)/shard_map/div | solution.py:36
  58.0 528.4 %while.14 = (s32[]{:T(128)}, f32[4,262144]{1,0:T(4,128)}, f32[4,262144]{1,0:T(4,128)}, f32[262144]{0:T(1024)S(1)}, f32[]{:T(128)}, /*index=5*/f32[]{:T(128)}, s32[]{:T(128)}) while((s32[]{:T(128)}, f32[4,262144]{1,0:T(4,128)}, f32[4,262144]{1,0:T(4,128)}, f32[262144]{0:T(1024)S(1)}, f32[]{:T(128)}, /*index=5*/f32[]{:T(128)}, s32[]{:T(128)}) %tuple.84), condition=%wide.region_1.2_spmd, body=%wide.region_0.1_spmd.sunk | while | flops 28311552 | bytes 190840976 | solution.py:43
  58.3 4.6 copy.33
  81.5 20.9 %divide_subtract_fusion.2 = f32[4,262144]{1,0:T(4,128)S(1)} fusion(f32[4,262144]{1,0:T(4,128)S(1)} %copy-done.3, f32[4,262144]{1,0:T(4,128)S(1)} %copy-done, f32[4,1]{1,0:T(4,128)S(1)} %get-tuple-element.222, f32[4,262143]{1,0:T(4,128)} %get-tuple-element.223, f32[4,262081]{1,0:T(4,128)} %get-tuple-element.224, f32[4,63]{1,0:T(4,128)S(1)} %get-tuple-element.225, ...), kind=kLoop, calls=%fused_computation.clone.1 | loop fusion | flops 23068672 | bytes 43515912 | tf_op jit(solution)/shard_map/while/body/eval_jaxpr/sub | solution.py:40
  129.5 20.9 %divide_subtract_fusion.2 = f32[4,262144]{1,0:T(4,128)S(1)} fusion(f32[4,262144]{1,0:T(4,128)S(1)} %copy-done.3, f32[4,262144]{1,0:T(4,128)S(1)} %copy-done, f32[4,1]{1,0:T(4,128)S(1)} %get-tuple-element.222, f32[4,262143]{1,0:T(4,128)} %get-tuple-element.223, f32[4,262081]{1,0:T(4,128)} %get-tuple-element.224, f32[4,63]{1,0:T(4,128)S(1)} %get-tuple-element.225, ...), kind=kLoop, calls=%fused_computation.clone.1 | loop fusion | flops 23068672 | bytes 43515912 | tf_op jit(solution)/shard_map/while/body/eval_jaxpr/sub | solution.py:40
  154.3 4.6 copy.33
  177.5 20.9 %divide_subtract_fusion.2 = f32[4,262144]{1,0:T(4,128)S(1)} fusion(f32[4,262144]{1,0:T(4,128)S(1)} %copy-done.3, f32[4,262144]{1,0:T(4,128)S(1)} %copy-done, f32[4,1]{1,0:T(4,128)S(1)} %get-tuple-element.222, f32[4,262143]{1,0:T(4,128)} %get-tuple-element.223, f32[4,262081]{1,0:T(4,128)} %get-tuple-element.224, f32[4,63]{1,0:T(4,128)S(1)} %get-tuple-element.225, ...), kind=kLoop, calls=%fused_computation.clone.1 | loop fusion | flops 23068672 | bytes 43515912 | tf_op jit(solution)/shard_map/while/body/eval_jaxpr/sub | solution.py:40
  202.3 4.6 copy.33
  225.5 20.9 %divide_subtract_fusion.2 = f32[4,262144]{1,0:T(4,128)S(1)} fusion(f32[4,262144]{1,0:T(4,128)S(1)} %copy-done.3, f32[4,262144]{1,0:T(4,128)S(1)} %copy-done, f32[4,1]{1,0:T(4,128)S(1)} %get-tuple-element.222, f32[4,262143]{1,0:T(4,128)} %get-tuple-element.223, f32[4,262081]{1,0:T(4,128)} %get-tuple-element.224, f32[4,63]{1,0:T(4,128)S(1)} %get-tuple-element.225, ...), kind=kLoop, calls=%fused_computation.clone.1 | loop fusion | flops 23068672 | bytes 43515912 | tf_op jit(solution)/shard_map/while/body/eval_jaxpr/sub | solution.py:40
  273.5 20.9 %divide_subtract_fusion.2 = f32[4,262144]{1,0:T(4,128)S(1)} fusion(f32[4,262144]{1,0:T(4,128)S(1)} %copy-done.3, f32[4,262144]{1,0:T(4,128)S(1)} %copy-done, f32[4,1]{1,0:T(4,128)S(1)} %get-tuple-element.222, f32[4,262143]{1,0:T(4,128)} %get-tuple-element.223, f32[4,262081]{1,0:T(4,128)} %get-tuple-element.224, f32[4,63]{1,0:T(4,128)S(1)} %get-tuple-element.225, ...), kind=kLoop, calls=%fused_computation.clone.1 | loop fusion | flops 23068672 | bytes 43515912 | tf_op jit(solution)/shard_map/while/body/eval_jaxpr/sub | solution.py:40
  321.4 20.9 %divide_subtract_fusion.2 = f32[4,262144]{1,0:T(4,128)S(1)} fusion(f32[4,262144]{1,0:T(4,128)S(1)} %copy-done.3, f32[4,262144]{1,0:T(4,128)S(1)} %copy-done, f32[4,1]{1,0:T(4,128)S(1)} %get-tuple-element.222, f32[4,262143]{1,0:T(4,128)} %get-tuple-element.223, f32[4,262081]{1,0:T(4,128)} %get-tuple-element.224, f32[4,63]{1,0:T(4,128)S(1)} %get-tuple-element.225, ...), kind=kLoop, calls=%fused_computation.clone.1 | loop fusion | flops 23068672 | bytes 43515912 | tf_op jit(solution)/shard_map/while/body/eval_jaxpr/sub | solution.py:40
  369.4 20.9 %divide_subtract_fusion.2 = f32[4,262144]{1,0:T(4,128)S(1)} fusion(f32[4,262144]{1,0:T(4,128)S(1)} %copy-done.3, f32[4,262144]{1,0:T(4,128)S(1)} %copy-done, f32[4,1]{1,0:T(4,128)S(1)} %get-tuple-element.222, f32[4,262143]{1,0:T(4,128)} %get-tuple-element.223, f32[4,262081]{1,0:T(4,128)} %get-tuple-element.224, f32[4,63]{1,0:T(4,128)S(1)} %get-tuple-element.225, ...), kind=kLoop, calls=%fused_computation.clone.1 | loop fusion | flops 23068672 | bytes 43515912 | tf_op jit(solution)/shard_map/while/body/eval_jaxpr/sub | solution.py:40
  417.4 20.9 %divide_subtract_fusion.2 = f32[4,262144]{1,0:T(4,128)S(1)} fusion(f32[4,262144]{1,0:T(4,128)S(1)} %copy-done.3, f32[4,262144]{1,0:T(4,128)S(1)} %copy-done, f32[4,1]{1,0:T(4,128)S(1)} %get-tuple-element.222, f32[4,262143]{1,0:T(4,128)} %get-tuple-element.223, f32[4,262081]{1,0:T(4,128)} %get-tuple-element.224, f32[4,63]{1,0:T(4,128)S(1)} %get-tuple-element.225, ...), kind=kLoop, calls=%fused_computation.clone.1 | loop fusion | flops 23068672 | bytes 43515912 | tf_op jit(solution)/shard_map/while/body/eval_jaxpr/sub | solution.py:40
  442.2 4.6 copy.33
  465.4 20.9 %divide_subtract_fusion.2 = f32[4,262144]{1,0:T(4,128)S(1)} fusion(f32[4,262144]{1,0:T(4,128)S(1)} %copy-done.3, f32[4,262144]{1,0:T(4,128)S(1)} %copy-done, f32[4,1]{1,0:T(4,128)S(1)} %get-tuple-element.222, f32[4,262143]{1,0:T(4,128)} %get-tuple-element.223, f32[4,262081]{1,0:T(4,128)} %get-tuple-element.224, f32[4,63]{1,0:T(4,128)S(1)} %get-tuple-element.225, ...), kind=kLoop, calls=%fused_computation.clone.1 | loop fusion | flops 23068672 | bytes 43515912 | tf_op jit(solution)/shard_map/while/body/eval_jaxpr/sub | solution.py:40
  513.4 20.9 %divide_subtract_fusion.2 = f32[4,262144]{1,0:T(4,128)S(1)} fusion(f32[4,262144]{1,0:T(4,128)S(1)} %copy-done.3, f32[4,262144]{1,0:T(4,128)S(1)} %copy-done, f32[4,1]{1,0:T(4,128)S(1)} %get-tuple-element.222, f32[4,262143]{1,0:T(4,128)} %get-tuple-element.223, f32[4,262081]{1,0:T(4,128)} %get-tuple-element.224, f32[4,63]{1,0:T(4,128)S(1)} %get-tuple-element.225, ...), kind=kLoop, calls=%fused_computation.clone.1 | loop fusion | flops 23068672 | bytes 43515912 | tf_op jit(solution)/shard_map/while/body/eval_jaxpr/sub | solution.py:40
  561.4 20.9 %divide_subtract_fusion.2 = f32[4,262144]{1,0:T(4,128)S(1)} fusion(f32[4,262144]{1,0:T(4,128)S(1)} %copy-done.3, f32[4,262144]{1,0:T(4,128)S(1)} %copy-done, f32[4,1]{1,0:T(4,128)S(1)} %get-tuple-element.222, f32[4,262143]{1,0:T(4,128)} %get-tuple-element.223, f32[4,262081]{1,0:T(4,128)} %get-tuple-element.224, f32[4,63]{1,0:T(4,128)S(1)} %get-tuple-element.225, ...), kind=kLoop, calls=%fused_computation.clone.1 | loop fusion | flops 23068672 | bytes 43515912 | tf_op jit(solution)/shard_map/while/body/eval_jaxpr/sub | solution.py:40
  586.3 4.6 copy.29
  609.9 23.3 %fusion.27 = f32[4,262144]{1,0:T(4,128)S(1)} fusion(f32[4,262144]{1,0:T(4,128)S(1)} %bitcast.66, f32[4,258048]{1,0:T(4,128)} %get-tuple-element.142, f32[4,4096]{1,0:T(4,128)S(1)} %get-tuple-element.144, f32[4,4096]{1,0:T(4,128)S(1)} %get-tuple-element.143, f32[4,258048]{1,0:T(4,128)} %get-tuple-element.141, f32[4,63]{1,0:T(4,128)S(1)} %get-tuple-element.138, ...), kind=kLoop, calls=%fused_computation.44 | loop fusion | flops 17825792 | bytes 39321600 | tf_op jit(solution)/shard_map/add | solution.py:30
  633.2 101.2 %all_to_all.38 = f32[4,32,8192]{2,0,1:T(4,128)} all-to-all(f32[4,32,8192]{2,0,1:T(4,128)S(1)} %bitcast.67), channel_id=1, replica_groups=mesh['ob'=8,'pt'=4] {'ob','pt'}, dimensions={1} | all-to-all | bytes 8388608 | tf_op jit(solution)/shard_map/all_to_all | solution.py:56
  738.0 5.5 all_to_all.35
  743.6 88.6 %all-to-all-done = f32[4,32,8192]{2,0,1:T(4,128)} async-done(((f32[4,32,8192]{2,0,1:T(4,128)}), f32[4,32,8192]{2,0,1:T(4,128)}, u32[]{:S(2)}, u32[]{:S(2)}) %all-to-all-start) | async-done | bytes 4194336 | tf_op jit(solution)/shard_map/all_to_all | solution.py:55
  832.1 5.3 all_to_all.31
  837.4 7.7 convolution_multiply_fusion.1
  849.3 9.9 convolution_bitcast_fusion.1
  859.1 5.6 copy.17
  864.7 110.7 %all-reduce.6.cloned.1.call-done = (f32[128,128]{1,0:T(8,128)}, f32[128,128]{1,0:T(8,128)}) async-done(((f32[128,128]{1,0:T(8,128)}, f32[128,128]{1,0:T(8,128)}), (f32[128,128]{1,0:T(8,128)}, f32[128,128]{1,0:T(8,128)})) %all-reduce.6.cloned.1.call-update) | async-done | bytes 131088
  977.1 39.6 %all-reduce.2 = (f32[128]{0:T(128)S(1)}, f32[128]{0:T(128)S(1)}) all-reduce(f32[128]{0:T(128)S(1)} %fusion.30, f32[128]{0:T(128)S(1)} %fusion.31), channel_id=1, replica_groups=mesh['ob'=8,'pt'=4] {'ob','pt'}, use_global_device_ids=true, to_apply=%region_5.6 | all-reduce | flops 256 | bytes 2048 | tf_op jit(solution)/shard_map/psum | solution.py:70
  1016.7 10.5 %fusion.13 = f32[128,8192]{0,1:T(8,128)} fusion(f32[128,8192]{1,0:T(8,128)} %all_to_all.35, f32[128,128]{1,0:T(8,128)S(1)} %copy-done.12, f32[128,8192]{0,1:T(8,128)} %convolution_bitcast_fusion.1, f32[128]{0:T(128)S(1)} %add_divide_fusion), kind=kOutput, calls=%fused_computation.22 | convolution fusion | flops 1612709888 | bytes 12648960 | tf_op jit(solution)/shard_map/dot_general | solution.py:65
  1027.2 5.6 copy.18
  (252 shorter events, 323.4 us)
Async XLA Ops:
  9.4 16.8 %copy-start.2 = (f32[4,262144]{1,0:T(4,128)}, f32[4,262144]{1,0:T(4,128)S(1)}, u32[]{:S(2)}) copy-start(f32[4,262144]{1,0:T(4,128)S(1)} %copy.48) | copy-start | bytes 12582916
  26.6 6.7 copy-start.8
  26.6 6.7 copy-start.10
  28.6 4.7 copy-start.5
  65.9 2.7 copy-start
  76.9 4.6 copy-start.3
  113.9 2.7 copy-start
  124.8 4.6 copy-start.3
  161.9 2.7 copy-start
  172.8 4.6 copy-start.3
  220.8 4.6 copy-start.3
  257.9 2.7 copy-start
  268.8 4.6 copy-start.3
  305.9 2.7 copy-start
  316.8 4.6 copy-start.3
  353.9 2.7 copy-start
  364.8 4.6 copy-start.3
  412.8 4.6 copy-start.3
  460.7 4.6 copy-start.3
  508.7 4.6 copy-start.3
  556.7 4.6 copy-start.3
  607.1 2.7 copy-start.7
  607.1 2.7 copy-start.9
  607.1 2.7 copy-start.11
  734.4 97.7 %all-to-all-start = ((f32[4,32,8192]{2,0,1:T(4,128)}), f32[4,32,8192]{2,0,1:T(4,128)}, u32[]{:S(2)}, u32[]{:S(2)}) async-start(f32[4,32,8192]{2,0,1:T(4,128)} %bitcast.55), calls=%async_computation | async-start | bytes 8388608 | tf_op jit(solution)/shard_map/all_to_all | solution.py:55
  738.0 237.4 %all-reduce.6.cloned.1.call-start = ((), (), s32[]{:S(2)}) async-start(), calls=%async_computation.2 | async-start | bytes 262144
  837.4 7.7 copy-start.4
  837.4 7.7 copy-start.6
  845.1 4.1 copy-start.12
  976.1 51.1 %copy-start.13 = (f32[4,128]{1,0:T(4,128)}, f32[4,128]{1,0:T(4,128)S(1)}, u32[]{:S(2)}) copy-start(f32[4,128]{1,0:T(4,128)S(1)} %constant_dynamic-slice_fusion) | copy-start | bytes 6148
  976.8 50.5 %copy-start.14 = (f32[4,128]{1,0:T(4,128)}, f32[4,128]{1,0:T(4,128)S(1)}, u32[]{:S(2)}) copy-start(f32[4,128]{1,0:T(4,128)S(1)} %constant_dynamic-slice_fusion.1) | copy-start | bytes 6148
  1016.7 10.5 %copy-start.15 = (f32[128]{0:T(128)}, f32[128]{0:T(128)S(1)}, u32[]{:S(2)}) copy-start(f32[128]{0:T(128)S(1)} %add_divide_fusion) | copy-start | bytes 1540
  (6 other events, 15.8 us)
Sparse Core Ops, SparseCore 0:
  849.4 125.9 all-reduce.5
where the time goes:
time: 1040 us
  local copies, waits for them, and re-layouts  349 us (34%)
  other arithmetic  299 us (29%)
  waiting for transfers between devices  199 us (19%)
  blocking collectives  141 us (14%)
  matrix products  32.6 us (3%)
  between operations  15.2 us (1%)
    sub x11, other arithmetic, advance(): 2.0 * (apply_ham(present, potential) - center * present) / half_width  229 us
    while x88, local copies, waits for them, and re-layouts  124 us
    unnamed x2, waiting for transfers between devices  111 us
    all_to_all x1, blocking collectives, on_device(): lax.all_to_all(applied, ('ob', 'pt'), split_axis=1, concat_axis=0, tiled=...  101 us
    all_to_all x1, waiting for transfers between devices, on_device(): lax.all_to_all(filtered, ('ob', 'pt'), split_axis=1, concat_axis=0, tiled...  88.6 us
    slice x24, local copies, waits for them, and re-layouts, apply_ham(): jnp.roll(fields, 1 - G, axis=-1)  54.5 us
    slice x24, local copies, waits for them, and re-layouts, apply_ham(): jnp.roll(fields, plane_len, axis=-1) + jnp.roll(fields, -plane_len, axis=-1)  49.1 us
    slice x24, local copies, waits for them, and re-layouts, apply_ham(): jnp.roll(fields, 1, axis=-1)  46.4 us
  transfers between devices with their start and end apart: 2, of which 2 were waited for; matrix products, arithmetic and copies ran while one was open for 1% of the time, Pallas kernels for 0%

commit v1 on v0

v1 whole, which is shorter than its diff:
```python
import functools

import jax
import jax.numpy as jnp
from jax import lax
from jax.experimental import pallas as pl
from jax.experimental.pallas import tpu as pltpu
from jax.sharding import PartitionSpec as P

G = 64
DEGREE = 12
LANES = 128
upper_bound = 8.0
quot_eps = 1e-06


def stencil_masks(shape):
    lane = lax.broadcasted_iota(jnp.int32, shape, 2)
    sub = lax.broadcasted_iota(jnp.int32, shape, 1)
    high_lane = lane >= G
    z_coord = lane % G
    low_sub = sub < 4
    return (
        high_lane & ~low_sub,
        ~high_lane & low_sub,
        z_coord == G - 1,
        z_coord == 0,
    )


def neighbour_sum(v, x_lower, x_upper, masks):
    m_up, m_down, m_last, m_first = masks
    w = pltpu.roll(v, G, 2)
    r = pltpu.roll(w, 4, 1)
    above = jnp.concatenate([r[1:], r[:1]], axis=0)
    below = jnp.concatenate([r[-1:], r[:-1]], axis=0)
    t = jnp.where(m_up, above, jnp.where(m_down, below, r))
    z_lower = pltpu.roll(jnp.where(m_last, w, v), 1, 2)
    z_upper = pltpu.roll(jnp.where(m_first, w, v), LANES - 1, 2)
    return (x_lower + x_upper) + (w + t) + (z_lower + z_upper)


def filter_kernel(cut_ref, pot_ref, orb_ref, filt_ref, appl_ref, coef_ref, sem):
    blocks = filt_ref.shape[0]
    plane = blocks // G
    cut = cut_ref[0]
    center = 0.5 * (upper_bound + cut)
    half_width = 0.5 * (upper_bound - cut)
    inv = 1.0 / half_width
    copy = pltpu.make_async_copy(orb_ref, filt_ref, sem)
    copy.start()

    def prep(x, c):
        rows = pl.ds(x * plane, plane)
        coef_ref[rows] = (2.0 * inv) * (pot_ref[rows] + (3.0 - center))
        return c

    lax.fori_loop(0, G, prep, 0)
    copy.wait()
    masks = stencil_masks((plane, 8, LANES))

    def sweep(cur, dst, kind):
        def body(x, c):
            here = pl.ds(x * plane, plane)
            down = pl.ds(jnp.where(x == 0, G - 1, x - 1) * plane, plane)
            up = pl.ds(jnp.where(x == G - 1, 0, x + 1) * plane, plane)
            v = cur[here]
            g = coef_ref[here] * v - inv * neighbour_sum(v, cur[down], cur[up], masks)
            if kind == 0:
                dst[here] = 0.5 * g
            elif kind == 1:
                dst[here] = g - dst[here]
            else:
                dst[here] = (0.5 * half_width) * g + center * v
            return c

        lax.fori_loop(0, G, body, 0)

    sweep(filt_ref, appl_ref, 0)

    def pair(j, c):
        sweep(appl_ref, filt_ref, 1)
        sweep(filt_ref, appl_ref, 1)
        return c

    lax.fori_loop(0, (DEGREE - 2) // 2, pair, 0)
    sweep(appl_ref, filt_ref, 1)
    sweep(filt_ref, appl_ref, 2)


def chebyshev(flat, pot, cutoff):
    vmem = pl.BlockSpec(memory_space=pltpu.VMEM)
    return pl.pallas_call(
        filter_kernel,
        out_shape=(
            jax.ShapeDtypeStruct(flat.shape, jnp.float32),
            jax.ShapeDtypeStruct(flat.shape, jnp.float32),
        ),
        in_specs=[
            pl.BlockSpec(memory_space=pltpu.SMEM),
            vmem,
            pl.BlockSpec(memory_space=pl.ANY),
        ],
        out_specs=(vmem, vmem),
        scratch_shapes=[pltpu.VMEM(flat.shape, jnp.float32), pltpu.SemaphoreType.DMA],
        compiler_params=pltpu.CompilerParams(vmem_limit_bytes=48 * 2**20),
        name="filter",
    )(cutoff, pot, flat)


def on_device(orbitals, potential, cutoff, eigvec):
    axes = ("ob", "pt")
    total_orb = eigvec.shape[0]
    n_dev = lax.axis_size("ob") * lax.axis_size("pt")
    per_dev, npts = orbitals.shape
    tiles = npts // LANES
    flat = orbitals.reshape(per_dev, tiles, LANES).transpose(1, 0, 2).reshape(-1, 8, LANES)
    pot = jnp.broadcast_to(
        potential.reshape(tiles, 1, LANES), (tiles, per_dev, LANES)
    ).reshape(-1, 8, LANES)
    filtered, applied = chebyshev(flat, pot, cutoff)

    def spread(a):
        a = a.reshape(n_dev, tiles // n_dev * per_dev, LANES)
        a = lax.all_to_all(a, axes, split_axis=0, concat_axis=0, tiled=True)
        a = a.reshape(n_dev, tiles // n_dev, per_dev, LANES)
        return a.transpose(0, 2, 1, 3).reshape(total_orb, npts // n_dev)

    filt, appl = spread(filtered), spread(applied)
    dot = functools.partial(jnp.dot, precision=lax.Precision.HIGH)
    part_gram = dot(filt, filt.T) / npts
    part_hamil = dot(filt, appl.T) / npts
    gram, hamil_sub = (
        lax.psum_scatter(part_gram, axes, scatter_dimension=0, tiled=True),
        lax.psum_scatter(part_hamil, axes, scatter_dimension=0, tiled=True),
    )
    rotated = dot(eigvec.T, filt)
    rot_applied = dot(eigvec.T, appl)
    numer = jnp.sum(rotated * rot_applied, axis=1) / npts
    denom = jnp.sum(rotated * rotated, axis=1) / npts
    numer, denom = lax.psum((numer, denom), axes)
    ritz = numer / (denom + quot_eps)
    residual = rot_applied - ritz[:, None] * rotated
    return (gram, hamil_sub, rotated, residual, ritz)


def solution(mesh):
    return jax.shard_map(
        on_device,
        mesh=mesh,
        in_specs=(P(("ob", "pt"), None), P(), P(), P()),
        out_specs=(
            P(("ob", "pt"), None),
            P(("ob", "pt"), None),
            P(None, ("ob", "pt")),
            P(None, ("ob", "pt")),
            P(),
        ),
        check_vma=False,
    )
```

time: 1040 us -> 538 us (0.52)
  local copies, waits for them, and re-layouts: 349 us -> 34 us
  other arithmetic: 299 us -> 5.85 us
  Pallas kernels: 0 us -> 152 us
  waiting for transfers between devices: 199 us -> 154 us
    sub x11 -> x1, other arithmetic: 229 us -> 5.84 us  [on_device(): residual = rot_applied - ritz[:, None] * rotated]
    slice x104 -> x0, local copies, waits for them, and re-layouts: 184 us -> none  [the longest x24 54.5 us: apply_ham(): jnp.roll(fields, 1 - G, axis=-1)]
    pallas_call x0 -> x1, Pallas kernels: none -> 152 us  [chebyshev(): pl.pallas_call(filter_kernel, out_shape=(jax.ShapeDtypeStruct(flat.shape,...]
    while x88 -> x0, local copies, waits for them, and re-layouts: 124 us -> none
    unnamed x2, waiting for transfers between devices: 111 us -> 69.2 us
    div x1, other arithmetic: 24.7 us -> 0.01 us  [on_device(): denom = jnp.sum(rotated * rotated, axis=1) / npts]
    add x1 -> x0, other arithmetic: 23.3 us -> none  [apply_ham(): -0.5 * (x_pair + y_pair + z_lower + z_upper - 6.0 * fields)]
    unnamed x37 -> x17, local copies, waits for them, and re-layouts: 29.7 us -> 14.5 us
  transfers between devices with their start and end apart: 2 -> 2, of which waited for: 2 -> 2; matrix products, arithmetic and copies ran while one was open for 1% -> 5% of each run, Pallas kernels for 0% -> 0%
where the time goes in v1:
time: 538 us; the launch traced here: 537 us
  waiting for transfers between devices  154 us (29%)
  Pallas kernels  152 us (28%)
  blocking collectives  141 us (26%)
  local copies, waits for them, and re-layouts  34 us (6%)
  matrix products  31.2 us (6%)
  between operations  14.8 us (3%)
  other arithmetic  5.85 us (1%)
    pallas_call x1, Pallas kernels, chebyshev(): pl.pallas_call(filter_kernel, out_shape=(jax.ShapeDtypeStruct(flat.shape,...  152 us
    all_to_all x1, blocking collectives, spread(): a = lax.all_to_all(a, axes, split_axis=0, concat_axis=0, tiled=True)  101 us
    all_to_all x1, waiting for transfers between devices, spread(): a = lax.all_to_all(a, axes, split_axis=0, concat_axis=0, tiled=True)  85 us
    unnamed x2, waiting for transfers between devices  69.2 us
    psum x1, blocking collectives, on_device(): numer, denom = lax.psum((numer, denom), axes)  39.9 us
    unnamed x17, local copies, waits for them, and re-layouts  14.5 us
  transfers between devices with their start and end apart: 2, of which 2 were waited for; matrix products, arithmetic and copies ran while one was open for 5% of the time, Pallas kernels for 0%

profile of v1, /device:TPU:0, one launch (start us, length us, event | category | flops | bytes accessed | tf_op | source)
XLA Modules:
  0.0 537.4 jit_solution(10681905066021254775)
XLA Ops:
  7.2 0.0 copy-start
  7.9 3.4 broadcast_in_dim.9
  11.3 152.3 %filter.1 = (f32[1024,8,128]{2,1,0:T(8,128)S(1)}, f32[1024,8,128]{2,1,0:T(8,128)}) custom-call(f32[1]{0:T(128)S(6)} %copy.61.cut_ref, f32[1024,8,128]{2,1,0:T(8,128)} %bitcast.51, f32[1024,8,128]{2,1,0:T(8,128)} %bitcast.54), custom_call_target="tpu_custom_call" | custom-call | tf_op jit(solution)/shard_map/filter/pallas_call | solution.py:93
  163.6 0.0 copy-start.1
  163.6 101.4 %all_to_all.10 = f32[32,256,128]{2,1,0:T(8,128)} all-to-all(f32[32,256,128]{2,1,0:T(8,128)} %bitcast.55), channel_id=1, replica_groups=mesh['ob'=8,'pt'=4] {'ob','pt'}, dimensions={0} | all-to-all | bytes 8388608 | tf_op jit(solution)/shard_map/all_to_all | solution.py:125
  265.0 0.0 copy-done.1
  265.0 3.6 all-to-all-start
  268.6 0.0 all-reduce.6.cloned.1.call-start
  268.7 4.6 copy.25
  273.3 4.4 copy.26
  277.7 85.0 %all-to-all-done = f32[32,256,128]{2,1,0:T(8,128)} async-done(((f32[32,256,128]{2,1,0:T(8,128)}), f32[32,256,128]{2,1,0:T(8,128)}, u32[]{:S(2)}, u32[]{:S(2)}) %all-to-all-start) | async-done | bytes 4194336 | tf_op jit(solution)/shard_map/all_to_all | solution.py:125
  362.8 4.6 copy.23
  367.4 2.4 copy.24
  369.8 0.0 copy-start.2
  369.8 0.0 copy-start.5
  369.8 7.7 %fusion.12 = f32[128,128]{1,0:T(8,128)} fusion(f32[16,8,64,128]{3,2,1,0:T(8,128)S(1)} %bitcast.46), kind=kOutput, calls=%fused_computation.17 | convolution fusion | flops 805322752 | bytes 4259840 | tf_op jit(solution)/shard_map/dot_general | solution.py:131
  377.5 0.0 copy-done.2
  377.5 0.0 copy-done.5
  377.5 7.7 %fusion.15 = f32[128,128]{1,0:T(8,128)} fusion(f32[16,8,64,128]{3,2,1,0:T(8,128)S(1)} %bitcast.50, f32[16,8,64,128]{3,2,1,0:T(8,128)S(1)} %bitcast.47), kind=kOutput, calls=%fused_computation.18 | convolution fusion | flops 805322752 | bytes 8454144 | tf_op jit(solution)/shard_map/dot_general | solution.py:132
  385.3 0.0 copy-done
  385.3 7.6 %convolution_bitcast_fusion = f32[128,8192]{0,1:T(8,128)S(1)} fusion(f32[128,128]{1,0:T(8,128)S(1)} %copy-done, f32[16,8,64,128]{3,2,1,0:T(8,128)} %bitcast.49), kind=kOutput, calls=%fused_computation | convolution fusion | flops 805306368 | bytes 8454144 | tf_op jit(solution)/shard_map/dot_general | solution.py:138
  392.9 0.0 copy-start.4
  392.9 2.0 copy-done.4
  394.9 0.0 copy-done.3
  394.9 8.2 %multiply_reduce_fusion = (f32[128]{0:T(128)S(1)}, f32[128]{0:T(128)S(1)}, f32[128,8192]{0,1:T(8,128)}) fusion(f32[128,8192]{0,1:T(8,128)S(1)} %convolution_bitcast_fusion, f32[128,128]{1,0:T(8,128)S(1)} %copy-done, f32[16,8,64,128]{3,2,1,0:T(8,128)S(1)} %bitcast.48), kind=kOutput, calls=%fused_computation.10 | convolution fusion | flops 809500416 | bytes 12649472 | tf_op jit(solution)/shard_map/dot_general | solution.py:137
  403.1 0.0 all-reduce.6.cloned.1.call-update
  403.1 39.9 %all-reduce.2 = (f32[128]{0:T(128)S(1)}, f32[128]{0:T(128)S(1)}) all-reduce(f32[128]{0:T(128)S(1)} %get-tuple-element.39, f32[128]{0:T(128)S(1)} %get-tuple-element.38), channel_id=1, replica_groups=mesh['ob'=8,'pt'=4] {'ob','pt'}, use_global_device_ids=true, to_apply=%region_3.0 | all-reduce | flops 256 | bytes 2048 | tf_op jit(solution)/shard_map/psum | solution.py:141
  443.0 5.8 %multiply_subtract_fusion = f32[128,8192]{0,1:T(8,128)} fusion(f32[128,8192]{0,1:T(8,128)} %copy-done.4, f32[128,8192]{0,1:T(8,128)} %get-tuple-element.35, f32[128]{0:T(128)S(1)} %add_divide_fusion), kind=kLoop, calls=%fused_computation.9 | loop fusion | flops 2097152 | bytes 12583424 | tf_op jit(solution)/shard_map/sub | solution.py:143
  448.8 5.6 %copy.27 = f32[128,8192]{1,0:T(8,128)} copy(f32[128,8192]{0,1:T(8,128)} %get-tuple-element.35) | data formatting | bytes 8388608
  454.4 5.6 %copy.28 = f32[128,8192]{1,0:T(8,128)} copy(f32[128,8192]{0,1:T(8,128)} %multiply_subtract_fusion) | data formatting | bytes 8388608
  460.0 69.2 %all-reduce.6.cloned.1.call-done = (f32[128,128]{1,0:T(8,128)}, f32[128,128]{1,0:T(8,128)}) async-done(((f32[128,128]{1,0:T(8,128)}, f32[128,128]{1,0:T(8,128)}), (f32[128,128]{1,0:T(8,128)}, f32[128,128]{1,0:T(8,128)})) %all-reduce.6.cloned.1.call-update) | async-done | bytes 131088
  529.3 1.3 constant_dynamic-slice_fusion
  (5 shorter events, 0.0 us)
Async XLA Ops:
  7.2 378.1 %copy-start = (f32[128,128]{1,0:T(8,128)S(1)}, f32[128,128]{1,0:T(8,128)}, u32[]{:S(2)}) copy-start(f32[128,128]{1,0:T(8,128)} %param.7) | copy-start | bytes 196612
  163.6 101.4 %copy-start.1 = (f32[1024,8,128]{2,1,0:T(8,128)}, f32[1024,8,128]{2,1,0:T(8,128)S(1)}, u32[]{:S(2)}) copy-start(f32[1024,8,128]{2,1,0:T(8,128)S(1)} %get-tuple-element.7) | copy-start | bytes 12582916
  265.0 97.7 %all-to-all-start = ((f32[32,256,128]{2,1,0:T(8,128)}), f32[32,256,128]{2,1,0:T(8,128)}, u32[]{:S(2)}, u32[]{:S(2)}) async-start(f32[32,256,128]{2,1,0:T(8,128)} %bitcast.45), calls=%async_computation | async-start | bytes 8388608 | tf_op jit(solution)/shard_map/all_to_all | solution.py:125
  268.6 260.6 %all-reduce.6.cloned.1.call-start = ((), (), s32[]{:S(2)}) async-start(), calls=%async_computation.2 | async-start | bytes 262144
  369.8 7.7 %copy-start.2 = (f32[32,4,64,128]{3,2,1,0:T(8,128)}, f32[32,4,64,128]{3,2,1,0:T(8,128)S(1)}, u32[]{:S(2)}) copy-start(f32[32,4,64,128]{3,2,1,0:T(8,128)S(1)} %copy.24) | copy-start | bytes 12582916
  369.8 7.7 %copy-start.5 = (f32[32,4,64,128]{3,2,1,0:T(8,128)S(1)}, f32[32,4,64,128]{3,2,1,0:T(8,128)}, u32[]{:S(2)}) copy-start(f32[32,4,64,128]{3,2,1,0:T(8,128)} %copy.26) | copy-start | bytes 12582916
  385.3 9.6 %copy-start.3 = (f32[32,4,64,128]{3,2,1,0:T(8,128)S(1)}, f32[32,4,64,128]{3,2,1,0:T(8,128)}, u32[]{:S(2)}) copy-start(f32[32,4,64,128]{3,2,1,0:T(8,128)} %copy-done.2) | copy-start | bytes 12582916
  392.9 2.0 copy-start.4
  443.0 5.8 %copy-start.6 = (f32[128]{0:T(128)}, f32[128]{0:T(128)S(1)}, u32[]{:S(2)}) copy-start(f32[128]{0:T(128)S(1)} %add_divide_fusion) | copy-start | bytes 1540
Sparse Core Ops, SparseCore 0:
  403.2 125.9 all-reduce.5

commit v2 on v1

v2 whole, which is shorter than its diff:
```python
import functools

import jax
import jax.numpy as jnp
from jax import lax
from jax.experimental import pallas as pl
from jax.experimental.pallas import tpu as pltpu
from jax.sharding import PartitionSpec as P

G = 64
DEGREE = 12
LANES = 128
UNROLL = 16
MESH = pl.DeviceIdType.MESH
upper_bound = 8.0
quot_eps = 1e-06


def shift_matrix():
    row = lax.broadcasted_iota(jnp.int32, (2 * LANES, 2 * LANES), 0) % LANES
    col = lax.broadcasted_iota(jnp.int32, (2 * LANES, 2 * LANES), 1)
    lane = col % LANES
    step = (row - lane) % G
    z_pair = (row // G == lane // G) & ((step == 1) | (step == G - 1))
    swap = (row + G) % LANES == lane
    return jnp.where(col < LANES, z_pair, swap).astype(jnp.bfloat16)


def split(x):
    hi = x.astype(jnp.bfloat16)
    return hi, (x - hi.astype(jnp.float32)).astype(jnp.bfloat16)


def row_masks():
    shape = (1, 8, LANES)
    high_lane = lax.broadcasted_iota(jnp.int32, shape, 2) >= G
    low_sub = lax.broadcasted_iota(jnp.int32, shape, 1) < 4
    return high_lane & ~low_sub, ~high_lane & low_sub


def neighbour_sum(v, x_lower, x_upper, masks, shifts):
    m_up, m_down = masks
    hi, lo = split(v.reshape(-1, LANES))
    both = jnp.dot(
        jnp.concatenate([hi, lo], axis=1), shifts, preferred_element_type=jnp.float32
    )
    z_pair = both[:, :LANES].reshape(v.shape)
    w = both[:, LANES:].reshape(v.shape)
    r = pltpu.roll(w, 4, 1)
    above = jnp.concatenate([r[1:], r[:1]], axis=0)
    below = jnp.concatenate([r[-1:], r[:-1]], axis=0)
    t = jnp.where(m_up, above, jnp.where(m_down, below, r))
    return (x_lower + x_upper) + (w + t) + z_pair


def run_filter(cut_ref, pot_ref, orb_ref, shift_ref, filt, spare, coef_ref, sem):
    plane = pot_ref.shape[0] // G
    cut = cut_ref[0]
    center = 0.5 * (upper_bound + cut)
    half_width = 0.5 * (upper_bound - cut)
    inv = 1.0 / half_width
    copy = pltpu.make_async_copy(orb_ref, filt, sem)
    copy.start()

    def prep(x, c):
        rows = pl.ds(x * plane, plane)
        coef_ref[rows] = (2.0 * inv) * (pot_ref[rows] + (3.0 - center))
        return c

    lax.fori_loop(0, G, prep, 0)
    copy.wait()
    masks = row_masks()

    def sweep(cur, dst, first):
        def one(x):
            here = pl.ds(x * plane, plane)
            down = pl.ds((x + G - 1) % G * plane, plane)
            up = pl.ds((x + 1) % G * plane, plane)
            v = cur[here]
            s = neighbour_sum(v, cur[down], cur[up], masks, shift_ref[...])
            g = coef_ref[here] * v - inv * s
            return here, 0.5 * g if first else g - dst[here]

        def body(i, c):
            for here, value in [one(i * UNROLL + u) for u in range(UNROLL)]:
                dst[here] = value
            return c

        lax.fori_loop(0, G // UNROLL, body, 0)

    sweep(filt, spare, True)

    def pair(j, c):
        sweep(spare, filt, False)
        sweep(filt, spare, False)
        return c

    lax.fori_loop(0, (DEGREE - 2) // 2, pair, 0)
    sweep(spare, filt, False)


def filter_kernel(cut_ref, pot_ref, orb_ref, shift_ref, filt_ref, appl_ref, coef_ref, sem):
    run_filter(cut_ref, pot_ref, orb_ref, shift_ref, filt_ref, appl_ref, coef_ref, sem)
    plane = pot_ref.shape[0] // G
    masks = row_masks()

    def body(i, c):
        for u in range(UNROLL):
            x = i * UNROLL + u
            here = pl.ds(x * plane, plane)
            down = pl.ds((x + G - 1) % G * plane, plane)
            up = pl.ds((x + 1) % G * plane, plane)
            v = filt_ref[here]
            s = neighbour_sum(v, filt_ref[down], filt_ref[up], masks, shift_ref[...])
            appl_ref[here] = (pot_ref[here] + 3.0) * v - 0.5 * s
        return c

    lax.fori_loop(0, G // UNROLL, body, 0)


def chebyshev(flat, pot, cutoff):
    vmem = pl.BlockSpec(memory_space=pltpu.VMEM)
    return pl.pallas_call(
        filter_kernel,
        out_shape=(
            jax.ShapeDtypeStruct(flat.shape, jnp.float32),
            jax.ShapeDtypeStruct(flat.shape, jnp.float32),
        ),
        in_specs=[
            pl.BlockSpec(memory_space=pltpu.SMEM),
            vmem,
            pl.BlockSpec(memory_space=pl.ANY),
            vmem,
        ],
        out_specs=(vmem, vmem),
        scratch_shapes=[pltpu.VMEM(flat.shape, jnp.float32), pltpu.SemaphoreType.DMA],
        compiler_params=pltpu.CompilerParams(vmem_limit_bytes=48 * 2**20),
        name="filter",
    )(cutoff, pot, flat, shift_matrix())


def dot3(a, b, contract):
    dims = ((contract[:1], contract[1:]), ((), ()))
    one = functools.partial(
        lax.dot_general, dimension_numbers=dims, preferred_element_type=jnp.float32
    )
    return one(a[0], b[0]) + (one(a[0], b[1]) + one(a[1], b[0]))


def rotate_kernel(eig_ref, filt_ref, appl_ref, rot_ref, rota_ref, gram_ref, hamil_ref, num_ref, den_ref):
    rows = num_ref.shape[0]

    @pl.when(pl.program_id(0) == 0)
    def _():
        gram_ref[...] = jnp.zeros_like(gram_ref)
        hamil_ref[...] = jnp.zeros_like(hamil_ref)
        num_ref[...] = jnp.zeros_like(num_ref)
        den_ref[...] = jnp.zeros_like(den_ref)

    eig = split(eig_ref[...])

    def body(b, c):
        f = split(filt_ref[:, b].reshape(2 * rows, LANES))
        a = split(appl_ref[:, b].reshape(2 * rows, LANES))
        gram_ref[...] += dot3(f, f, (1, 1))
        hamil_ref[...] += dot3(f, a, (1, 1))
        rot = dot3(eig, f, (1, 0))
        rota = dot3(eig, a, (1, 0))
        for par in range(2):
            cols = pl.ds(pl.multiple_of((2 * b + par) * LANES, LANES), LANES)
            x = rot[par * rows : (par + 1) * rows]
            y = rota[par * rows : (par + 1) * rows]
            rot_ref[:, cols] = x
            rota_ref[:, cols] = y
            num_ref[...] += x * y
            den_ref[...] += x * x
        return c

    lax.fori_loop(0, filt_ref.shape[1], body, 0)


def rotate(filt, appl, eigvec):
    rows = eigvec.shape[0]
    n_src, blocks = filt.shape[:2]
    per_dev = rows // n_src
    step = min(blocks, max(1, 8 * 128 // rows))
    parity = lax.broadcasted_iota(jnp.int32, (2 * rows, 1), 0) // per_dev % 2
    doubled = jnp.broadcast_to(
        eigvec.reshape(n_src, 1, per_dev, rows), (n_src, 2, per_dev, rows)
    ).reshape(2 * rows, rows)
    spread = jnp.concatenate(
        [jnp.where(parity == 0, doubled, 0.0), jnp.where(parity == 1, doubled, 0.0)], axis=1
    ).T
    f32 = lambda *s: jax.ShapeDtypeStruct(s, jnp.float32)
    whole = lambda *s: pl.BlockSpec(s, lambda i: (0,) * len(s))
    field = pl.BlockSpec((n_src, step, 8, LANES), lambda i: (0, i, 0, 0))
    out = pl.BlockSpec((rows, 2 * step * LANES), lambda i: (0, i))
    rot, rota, gram, hamil, num, den = pl.pallas_call(
        rotate_kernel,
        grid=(blocks // step,),
        out_shape=(
            f32(rows, 2 * blocks * LANES),
            f32(rows, 2 * blocks * LANES),
            f32(2 * rows, 2 * rows),
            f32(2 * rows, 2 * rows),
            f32(rows, LANES),
            f32(rows, LANES),
        ),
        in_specs=[whole(2 * rows, 2 * rows), field, field],
        out_specs=(
            out,
            out,
            whole(2 * rows, 2 * rows),
            whole(2 * rows, 2 * rows),
            whole(rows, LANES),
            whole(rows, LANES),
        ),
        compiler_params=pltpu.CompilerParams(vmem_limit_bytes=56 * 2**20),
        name="rotate",
    )(spread, filt, appl)

    def fold(m):
        m = jnp.where(parity == parity.T, m, 0.0)
        half = m.reshape(n_src, 2, per_dev, 2 * rows).sum(axis=1).reshape(rows, 2 * rows).T
        return half.reshape(n_src, 2, per_dev, rows).sum(axis=1).reshape(rows, rows).T

    return rot, rota, fold(gram), fold(hamil), num.sum(axis=1), den.sum(axis=1)


def reduce_kernel(n_ob, n_pt, part_ref, out_ref, recv, send_sem, recv_sem):
    n_dev = n_ob * n_pt
    me = lax.axis_index("ob") * n_pt + lax.axis_index("pt")
    barrier = pltpu.get_barrier_semaphore()

    def copy(k):
        to = (me + k) % n_dev
        return pltpu.make_async_remote_copy(
            src_ref=part_ref.at[to],
            dst_ref=recv.at[k],
            send_sem=send_sem.at[k],
            recv_sem=recv_sem.at[k],
            device_id=(to // n_pt, to % n_pt),
            device_id_type=MESH,
        )

    def greet(k, c):
        to = (me + k) % n_dev
        pl.semaphore_signal(
            barrier, inc=1, device_id=(to // n_pt, to % n_pt), device_id_type=MESH
        )
        return c

    def start(k, c):
        copy(k).start()
        return c

    def finish(k, total):
        copy(k).wait()
        return total + recv[k]

    lax.fori_loop(1, n_dev, greet, 0)
    pl.semaphore_wait(barrier, n_dev - 1)
    lax.fori_loop(1, n_dev, start, 0)
    out_ref[...] = lax.fori_loop(1, n_dev, finish, part_ref[me])


def reduce_parts(parts, n_ob, n_pt):
    n_dev, rows, cols = parts.shape
    vmem = pl.BlockSpec(memory_space=pltpu.VMEM)
    return pl.pallas_call(
        functools.partial(reduce_kernel, n_ob, n_pt),
        out_shape=jax.ShapeDtypeStruct((rows, cols), jnp.float32),
        in_specs=[vmem],
        out_specs=vmem,
        scratch_shapes=[
            pltpu.VMEM((n_dev, rows, cols), jnp.float32),
            pltpu.SemaphoreType.DMA((n_dev,)),
            pltpu.SemaphoreType.DMA((n_dev,)),
        ],
        compiler_params=pltpu.CompilerParams(
            collective_id=1, has_side_effects=True, vmem_limit_bytes=32 * 2**20
        ),
        name="reduce_parts",
    )(parts)


def on_device(orbitals, potential, cutoff, eigvec):
    axes = ("ob", "pt")
    total_orb = eigvec.shape[0]
    n_ob, n_pt = lax.axis_size("ob"), lax.axis_size("pt")
    n_dev = n_ob * n_pt
    per_dev, npts = orbitals.shape
    tiles = npts // LANES
    flat = orbitals.reshape(per_dev, tiles, LANES).transpose(1, 0, 2).reshape(-1, 8, LANES)
    pot = jnp.broadcast_to(
        potential.reshape(tiles, 1, LANES), (tiles, per_dev, LANES)
    ).reshape(-1, 8, LANES)
    filtered, applied = chebyshev(flat, pot, cutoff)

    def spread(a):
        a = a.reshape(n_dev, -1, LANES)
        a = lax.all_to_all(a, axes, split_axis=0, concat_axis=0, tiled=True)
        return a.reshape(n_dev, -1, 8, LANES)

    rotated, rot_applied, gram, hamil, numer, denom = rotate(
        spread(filtered), spread(applied), eigvec
    )
    quotient = jnp.broadcast_to(jnp.stack([numer, denom]), (n_dev, 2, total_orb))
    parts = jnp.concatenate(
        [
            gram.reshape(n_dev, per_dev, total_orb),
            hamil.reshape(n_dev, per_dev, total_orb),
            quotient,
            jnp.zeros((n_dev, -(2 * per_dev + 2) % 8, total_orb), jnp.float32),
        ],
        axis=1,
    )
    sums = reduce_parts(parts, n_ob, n_pt) / npts
    gram, hamil_sub = sums[:per_dev], sums[per_dev : 2 * per_dev]
    numer, denom = sums[2 * per_dev], sums[2 * per_dev + 1]
    ritz = numer / (denom + quot_eps)
    residual = rot_applied - ritz[:, None] * rotated
    return (gram, hamil_sub, rotated, residual, ritz)


def solution(mesh):
    return jax.shard_map(
        on_device,
        mesh=mesh,
        in_specs=(P(("ob", "pt"), None), P(), P(), P()),
        out_specs=(
            P(("ob", "pt"), None),
            P(("ob", "pt"), None),
            P(None, ("ob", "pt")),
            P(None, ("ob", "pt")),
            P(),
        ),
        check_vma=False,
    )
```

time: 538 us -> 286 us (0.53)
  Pallas kernels: 152 us -> 71.9 us
  waiting for transfers between devices: 154 us -> 93.1 us
  blocking collectives: 141 us -> 101 us
  matrix products: 31.2 us -> 0 us
  local copies, waits for them, and re-layouts: 34 us -> 4.83 us
  between operations: 14.8 us -> 1.55 us
    pallas_call x1, Pallas kernels: 152 us -> 38.8 us  [chebyshev(): pl.pallas_call(filter_kernel, out_shape=(jax.ShapeDtypeStruct(flat.shape,...]
    unnamed x2 -> x0, waiting for transfers between devices: 69.2 us -> none
    psum x1 -> x0, blocking collectives: 39.9 us -> none  [on_device(): numer, denom = lax.psum((numer, denom), axes)]
    pallas_call x0 -> x2, Pallas kernels: none -> 33.1 us  [the longest x1 22.1 us: rotate(): pl.pallas_call(rotate_kernel, grid=(blocks // step,), out_shape=(f32(rows...]
    dot_general x4 -> x0, matrix products: 31.2 us -> none  [the longest x1 8.21 us: on_device(): rotated = dot(eigvec.T, filt)]
    unnamed x17 -> x10, local copies, waits for them, and re-layouts: 14.5 us -> 0.03 us
    all_to_all x2 -> x0, local copies, waits for them, and re-layouts: 9.24 us -> none  [spread(): a = lax.all_to_all(a, axes, split_axis=0, concat_axis=0, tiled=True)]
    all_to_all x1, waiting for transfers between devices: 85 us -> 93.1 us  [spread(): a = lax.all_to_all(a, axes, split_axis=0, concat_axis=0, tiled=True)]
  transfers between devices with their start and end apart: 2 -> 1, of which waited for: 2 -> 1; matrix products, arithmetic and copies ran while one was open for 5% -> 0% of each run, Pallas kernels for 0% -> 0%
where the time goes in v2:
time: 286 us
  blocking collectives  101 us (35%)
  waiting for transfers between devices  93.1 us (33%)
  Pallas kernels  71.9 us (25%)
  other arithmetic  8.98 us (3%)
  local copies, waits for them, and re-layouts  4.83 us (2%)
  starting transfers between devices  3.7 us (1%)
    all_to_all x1, blocking collectives, spread(): a = lax.all_to_all(a, axes, split_axis=0, concat_axis=0, tiled=True)  101 us
    all_to_all x1, waiting for transfers between devices, spread(): a = lax.all_to_all(a, axes, split_axis=0, concat_axis=0, tiled=True)  93.1 us
    pallas_call x1, Pallas kernels, chebyshev(): pl.pallas_call(filter_kernel, out_shape=(jax.ShapeDtypeStruct(flat.shape,...  38.8 us
    pallas_call x1, Pallas kernels, rotate(): pl.pallas_call(rotate_kernel, grid=(blocks // step,), out_shape=(f32(rows...  22.1 us
    pallas_call x1, Pallas kernels, reduce_parts(): pl.pallas_call(functools.partial(reduce_kernel, n_ob, n_pt), out_shape=ja...  11 us
    sub x1, other arithmetic, on_device(): residual = rot_applied - ritz[:, None] * rotated  6.13 us
  transfers between devices with their start and end apart: 1, of which 1 were waited for; matrix products, arithmetic and copies ran while one was open for 0% of the time, Pallas kernels for 0%

profile of v2, /device:TPU:0, one launch (start us, length us, event | category | flops | bytes accessed | tf_op | source)
XLA Modules:
  0.0 285.6 jit_solution(3100802713454468039)
XLA Ops:
  1.3 0.4 fusion.21.shift_ref
  1.7 3.4 %broadcast_in_dim.50 = f32[2048,4,128]{2,1,0:T(4,128)} broadcast(f32[2048,128]{1,0:T(8,128)} %bitcast.36), dimensions={0,2} | broadcast | bytes 5242880 | tf_op jit(solution)/shard_map/broadcast_in_dim | solution.py:295
  5.1 38.8 %filter.1 = (f32[1024,8,128]{2,1,0:T(8,128)S(1)}, f32[1024,8,128]{2,1,0:T(8,128)}) custom-call(f32[1]{0:T(128)S(6)} %copy.23.cut_ref, f32[1024,8,128]{2,1,0:T(8,128)} %bitcast.32, f32[1024,8,128]{2,1,0:T(8,128)} %bitcast.34, bf16[256,256]{1,0:T(8,128)(2,1)S(1)} %fusion.21.shift_ref), custom_call_target="tpu_custom_call" | custom-call | tf_op jit(solution)/shard_map/filter/pallas_call | solution.py:123
  44.0 0.0 copy-start
  44.0 101.4 %all_to_all.10 = f32[32,256,128]{2,1,0:T(8,128)} all-to-all(f32[32,256,128]{2,1,0:T(8,128)} %bitcast.35), channel_id=1, replica_groups=mesh['ob'=8,'pt'=4] {'ob','pt'}, dimensions={0} | all-to-all | bytes 8388608 | tf_op jit(solution)/shard_map/all_to_all | solution.py:302
  145.4 0.0 copy-done
  145.4 3.7 %all-to-all-start = ((f32[32,256,128]{2,1,0:T(8,128)}), f32[32,256,128]{2,1,0:T(8,128)}, u32[]{:S(2)}, u32[]{:S(2)}) async-start(f32[32,256,128]{2,1,0:T(8,128)} %bitcast.31), calls=%async_computation | async-start | bytes 8388608 | tf_op jit(solution)/shard_map/all_to_all | solution.py:302
  149.1 0.0 copy-done.1
  149.2 0.1 copy.16
  149.3 0.1 pad.3.clone
  149.4 0.7 maximum_bitcast_fusion.eig_ref
  150.1 93.1 %all-to-all-done = f32[32,256,128]{2,1,0:T(8,128)} async-done(((f32[32,256,128]{2,1,0:T(8,128)}), f32[32,256,128]{2,1,0:T(8,128)}, u32[]{:S(2)}, u32[]{:S(2)}) %all-to-all-start) | async-done | bytes 4194336 | tf_op jit(solution)/shard_map/all_to_all | solution.py:302
  243.3 22.1 %rotate.1 = (f32[128,8192]{1,0:T(8,128)}, f32[128,8192]{1,0:T(8,128)}, f32[256,256]{1,0:T(8,128)}, f32[256,256]{1,0:T(8,128)}, f32[128,128]{1,0:T(8,128)}, /*index=5*/f32[128,128]{1,0:T(8,128)}) custom-call(f32[256,256]{1,0:T(8,128)} %maximum_bitcast_fusion.eig_ref, f32[32,32,8,128]{3,2,1,0:T(8,128)} %bitcast.9.filt_ref, f32[32,32,8,128]{3,2,1,0:T(8,128)} %bitcast.33), custom_call_target="tpu_custom_call" | custom-call | tf_op jit(solution)/shard_map/rotate/pallas_call | solution.py:198
  265.3 0.0 copy-start.3
  265.4 0.0 copy-start.2
  265.4 1.2 compare_select_fusion.1
  266.5 0.1 reshape.173
  266.6 0.1 reduce_sum.54
  266.8 0.1 copy.19
  266.9 0.1 copy.20
  267.0 0.1 reshape.178
  267.1 0.1 reduce_sum.56
  267.2 0.1 copy.21
  267.3 0.1 copy.22
  267.5 0.1 reduce_sum.58
  267.6 0.1 reduce_sum.59
  267.7 0.1 maximum_maximum_fusion.part_ref
  267.8 11.0 %reduce_parts.1 = f32[16,128]{1,0:T(8,128)S(1)} custom-call(f32[32,16,128]{2,1,0:T(8,128)S(1)} %maximum_maximum_fusion.part_ref), custom_call_target="tpu_custom_call" | custom-call | tf_op jit(solution)/shard_map/reduce_parts/pallas_call | solution.py:270
  278.8 0.0 copy-start.4
  278.9 0.6 fusion.26
  279.4 6.1 %multiply_subtract_fusion = f32[128,8192]{1,0:T(8,128)} fusion(f32[128,8192]{1,0:T(8,128)} %get-tuple-element.20, f32[128,8192]{1,0:T(8,128)} %get-tuple-element.10, f32[128]{0:T(128)S(1)} %fusion.25), kind=kLoop, calls=%fused_computation | loop fusion | flops 2097152 | bytes 12583424 | tf_op jit(solution)/shard_map/sub | solution.py:322
  285.6 0.0 copy-done.4
  (18 shorter events, 0.3 us)
Async XLA Ops:
  44.0 101.4 %copy-start = (f32[1024,8,128]{2,1,0:T(8,128)}, f32[1024,8,128]{2,1,0:T(8,128)S(1)}, u32[]{:S(2)}) copy-start(f32[1024,8,128]{2,1,0:T(8,128)S(1)} %get-tuple-element.13) | copy-start | bytes 12582916
  145.4 3.7 %copy-start.1 = (f32[128,128]{1,0:T(8,128)S(1)}, f32[128,128]{1,0:T(8,128)}, u32[]{:S(2)}) copy-start(f32[128,128]{1,0:T(8,128)} %param.7) | copy-start | bytes 196612
  145.4 97.8 %all-to-all-start = ((f32[32,256,128]{2,1,0:T(8,128)}), f32[32,256,128]{2,1,0:T(8,128)}, u32[]{:S(2)}, u32[]{:S(2)}) async-start(f32[32,256,128]{2,1,0:T(8,128)} %bitcast.31), calls=%async_computation | async-start | bytes 8388608 | tf_op jit(solution)/shard_map/all_to_all | solution.py:302
  265.3 2.1 copy-start.3
  265.4 2.2 copy-start.2
  278.8 6.7 %copy-start.4 = (f32[128]{0:T(128)}, f32[128]{0:T(128)S(1)}, u32[]{:S(2)}) copy-start(f32[128]{0:T(128)S(1)} %fusion.25) | copy-start | bytes 1540

commit v3 on v2

--- a/solution.py
+++ b/solution.py
@@ -99,42 +99,157 @@
     sweep(spare, filt, False)
 
 
-def filter_kernel(cut_ref, pot_ref, orb_ref, shift_ref, filt_ref, appl_ref, coef_ref, sem):
-    run_filter(cut_ref, pot_ref, orb_ref, shift_ref, filt_ref, appl_ref, coef_ref, sem)
-    plane = pot_ref.shape[0] // G
+def filter_kernel(n_ob, n_pt, cut_ref, pot_ref, orb_ref, shift_ref, filt_out, appl_out, ext, spare, coef_ref, zbuf, sem, zsend, zrecv, psend, precv, own_sem):
+    blocks = pot_ref.shape[0]
+    plane = blocks // G
+    outer = n_ob // 2
+    peers = 2 * n_pt
+    slab = blocks // outer
+    piece = slab // peers
+    ob, pt = lax.axis_index("ob"), lax.axis_index("pt")
+    group = ob // 2
+    seat = ob % 2 * n_pt + pt
+
+    def group_dev(d):
+        return ((group + d) % outer * 2 + ob % 2, pt)
+
+    def peer_dev(k):
+        to = (seat + k) % peers
+        return (group * 2 + to // n_pt, to % n_pt)
+
+    barrier = pltpu.get_barrier_semaphore()
+    for d in range(1, outer):
+        pl.semaphore_signal(barrier, inc=1, device_id=group_dev(d), device_id_type=MESH)
+    for k in range(1, peers):
+        pl.semaphore_signal(barrier, inc=1, device_id=peer_dev(k), device_id_type=MESH)
+
+    filt = ext.at[pl.ds(plane, blocks)]
+    run_filter(cut_ref, pot_ref, orb_ref, shift_ref, filt, spare, coef_ref, sem)
+    ext[pl.ds(0, plane)] = ext[pl.ds(blocks, plane)]
+    ext[pl.ds(plane + blocks, plane)] = ext[pl.ds(plane, plane)]
+    pl.semaphore_wait(barrier, outer + peers - 2)
+
+    def zcopy(d):
+        return pltpu.make_async_remote_copy(
+            src_ref=ext.at[pl.ds((group + d) % outer * slab, slab + 2 * plane)],
+            dst_ref=zbuf.at[d - 1],
+            send_sem=zsend.at[d],
+            recv_sem=zrecv.at[d],
+            device_id=group_dev(d),
+            device_id_type=MESH,
+        )
+
+    for d in range(1, outer):
+        zcopy(d).start()
     masks = row_masks()
-
-    def body(i, c):
-        for u in range(UNROLL):
-            x = i * UNROLL + u
-            here = pl.ds(x * plane, plane)
-            down = pl.ds((x + G - 1) % G * plane, plane)
-            up = pl.ds((x + 1) % G * plane, plane)
-            v = filt_ref[here]
-            s = neighbour_sum(v, filt_ref[down], filt_ref[up], masks, shift_ref[...])
-            appl_ref[here] = (pot_ref[here] + 3.0) * v - 0.5 * s
-        return c
-
-    lax.fori_loop(0, G // UNROLL, body, 0)
-
-
-def chebyshev(flat, pot, cutoff):
+    unroll = min(8, slab // plane)
+
+    def source(d):
+        return ext.at[pl.ds(group * slab, slab + 2 * plane)] if d == 0 else zbuf.at[d - 1]
+
+    def pcopies(d, k):
+        to = (seat + k) % peers
+        slot = (group + outer - d) % outer * peers + seat
+        srcs = (
+            source(d).at[pl.ds(plane + to * piece, piece)],
+            spare.at[pl.ds(d * slab + to * piece, piece)],
+        )
+        return [
+            pltpu.make_async_remote_copy(
+                src_ref=srcs[i],
+                dst_ref=out.at[slot],
+                send_sem=psend.at[d, k, i],
+                recv_sem=precv.at[d, k, i],
+                device_id=peer_dev(k),
+                device_id_type=MESH,
+            )
+            for i, out in enumerate((filt_out, appl_out))
+        ]
+
+    def own_copies(d):
+        slot = (group + outer - d) % outer * peers + seat
+        srcs = (
+            source(d).at[pl.ds(plane + seat * piece, piece)],
+            spare.at[pl.ds(d * slab + seat * piece, piece)],
+        )
+        return [
+            pltpu.make_async_copy(srcs[i], out.at[slot], own_sem.at[d, i])
+            for i, out in enumerate((filt_out, appl_out))
+        ]
+
+    for d in range(outer):
+        if d > 0:
+            zcopy(d).wait_recv()
+        src = source(d)
+
+        def body(i, c):
+            for u in range(unroll):
+                x = i * unroll + u
+                v = src[pl.ds((x + 1) * plane, plane)]
+                s = neighbour_sum(
+                    v,
+                    src[pl.ds(x * plane, plane)],
+                    src[pl.ds((x + 2) * plane, plane)],
+                    masks,
+                    shift_ref[...],
+                )
+                rows = pl.ds(group * slab + x * plane, plane)
+                spare[pl.ds(d * slab + x * plane, plane)] = (pot_ref[rows] + 3.0) * v - 0.5 * s
+            return c
+
+        lax.fori_loop(0, slab // plane // unroll, body, 0)
+
+        def send(k, c):
+            for copy in pcopies(d, k):
+                copy.start()
+            return c
+
+        lax.fori_loop(1, peers, send, 0)
+        for copy in own_copies(d):
+            copy.start()
+
+    for d in range(outer):
+
+        def finish(k, c):
+            for copy in pcopies(d, k):
+                copy.wait()
+            return c
+
+        lax.fori_loop(1, peers, finish, 0)
+        for copy in own_copies(d):
+            copy.wait()
+        if d > 0:
+            zcopy(d).wait_send()
+
+
+def chebyshev(flat, pot, cutoff, n_ob, n_pt):
     vmem = pl.BlockSpec(memory_space=pltpu.VMEM)
+    anywhere = pl.BlockSpec(memory_space=pl.ANY)
+    blocks = flat.shape[0]
+    outer, peers, plane = n_ob // 2, 2 * n_pt, blocks // G
+    slab = blocks // outer
+    result = jax.ShapeDtypeStruct((n_ob * n_pt, slab // peers, 8, LANES), jnp.float32)
+    dma = pltpu.SemaphoreType.DMA
     return pl.pallas_call(
-        filter_kernel,
-        out_shape=(
-            jax.ShapeDtypeStruct(flat.shape, jnp.float32),
-            jax.ShapeDtypeStruct(flat.shape, jnp.float32),
+        functools.partial(filter_kernel, n_ob, n_pt),
+        out_shape=(result, result),
+        in_specs=[pl.BlockSpec(memory_space=pltpu.SMEM), vmem, anywhere, vmem],
+        out_specs=(anywhere, anywhere),
+        scratch_shapes=[
+            pltpu.VMEM((blocks + 2 * plane, 8, LANES), jnp.float32),
+            pltpu.VMEM(flat.shape, jnp.float32),
+            pltpu.VMEM(flat.shape, jnp.float32),
+            pltpu.VMEM((outer - 1, slab + 2 * plane, 8, LANES), jnp.float32),
+            dma,
+            dma((outer,)),
+            dma((outer,)),
+            dma((outer, peers, 2)),
+            dma((outer, peers, 2)),
+            dma((outer, 2)),
+        ],
+        compiler_params=pltpu.CompilerParams(
+            collective_id=0, has_side_effects=True, vmem_limit_bytes=48 * 2**20
         ),
-        in_specs=[
-            pl.BlockSpec(memory_space=pltpu.SMEM),
-            vmem,
-            pl.BlockSpec(memory_space=pl.ANY),
-            vmem,
-        ],
-        out_specs=(vmem, vmem),
-        scratch_shapes=[pltpu.VMEM(flat.shape, jnp.float32), pltpu.SemaphoreType.DMA],
-        compiler_params=pltpu.CompilerParams(vmem_limit_bytes=48 * 2**20),
         name="filter",
     )(cutoff, pot, flat, shift_matrix())
 
@@ -295,16 +410,8 @@
     pot = jnp.broadcast_to(
         potential.reshape(tiles, 1, LANES), (tiles, per_dev, LANES)
     ).reshape(-1, 8, LANES)
-    filtered, applied = chebyshev(flat, pot, cutoff)
-
-    def spread(a):
-        a = a.reshape(n_dev, -1, LANES)
-        a = lax.all_to_all(a, axes, split_axis=0, concat_axis=0, tiled=True)
-        return a.reshape(n_dev, -1, 8, LANES)
-
-    rotated, rot_applied, gram, hamil, numer, denom = rotate(
-        spread(filtered), spread(applied), eigvec
-    )
+    filtered, applied = chebyshev(flat, pot, cutoff, n_ob, n_pt)
+    rotated, rot_applied, gram, hamil, numer, denom = rotate(filtered, applied, eigvec)
     quotient = jnp.broadcast_to(jnp.stack([numer, denom]), (n_dev, 2, total_orb))
     parts = jnp.concatenate(
         [

time: 286 us -> 238 us (0.83)
  Pallas kernels: 71.9 us -> 220 us
  blocking collectives: 101 us -> 0 us
  waiting for transfers between devices: 93.1 us -> 0 us
  starting transfers between devices: 3.7 us -> 0 us
    pallas_call x1, Pallas kernels: 38.8 us -> 164 us  [chebyshev(): pl.pallas_call(functools.partial(filter_kernel, n_ob, n_pt), out_shape=(r...]
    all_to_all x1 -> x0, blocking collectives: 101 us -> none  [spread(): a = lax.all_to_all(a, axes, split_axis=0, concat_axis=0, tiled=True)]
    all_to_all x1 -> x0, waiting for transfers between devices: 93.1 us -> none  [spread(): a = lax.all_to_all(a, axes, split_axis=0, concat_axis=0, tiled=True)]
    pallas_call x1, Pallas kernels: 11 us -> 33.5 us  [reduce_parts(): pl.pallas_call(functools.partial(reduce_kernel, n_ob, n_pt), out_shape=ja...]
    all_to_all x1 -> x0, starting transfers between devices: 3.7 us -> none  [spread(): a = lax.all_to_all(a, axes, split_axis=0, concat_axis=0, tiled=True)]
  transfers between devices with their start and end apart: 1 -> 0, of which waited for: 1 -> 0; matrix products, arithmetic and copies ran while one was open for 0% -> 0% of each run, Pallas kernels for 0% -> 0%
where the time goes in v3:
time: 238 us
  Pallas kernels  220 us (92%)
  other arithmetic  8.99 us (4%)
  local copies, waits for them, and re-layouts  7.67 us (3%)
    pallas_call x1, Pallas kernels, chebyshev(): pl.pallas_call(functools.partial(filter_kernel, n_ob, n_pt), out_shape=(r...  164 us
    pallas_call x1, Pallas kernels, reduce_parts(): pl.pallas_call(functools.partial(reduce_kernel, n_ob, n_pt), out_shape=ja...  33.5 us
    pallas_call x1, Pallas kernels, rotate(): pl.pallas_call(rotate_kernel, grid=(blocks // step,), out_shape=(f32(rows...  22.1 us
    sub x1, other arithmetic, on_device(): residual = rot_applied - ritz[:, None] * rotated  6.13 us

profile of v3, /device:TPU:0, one launch (start us, length us, event | category | flops | bytes accessed | tf_op | source)
XLA Modules:
  0.0 237.8 jit_solution(9140758294160604978)
XLA Ops:
  0.6 0.9 broadcast_in_dim.46
  1.5 0.1 copy.16
  1.6 0.7 maximum_bitcast_fusion.eig_ref
  2.4 0.4 fusion.21.shift_ref
  2.8 3.4 %broadcast_in_dim.50 = f32[2048,4,128]{2,1,0:T(4,128)} broadcast(f32[2048,128]{1,0:T(8,128)} %bitcast.29), dimensions={0,2} | broadcast | bytes 5242880 | tf_op jit(solution)/shard_map/broadcast_in_dim | solution.py:410
  6.9 164.0 %filter.1 = (f32[32,32,8,128]{3,2,1,0:T(8,128)S(1)}, f32[32,32,8,128]{3,2,1,0:T(8,128)}) custom-call(f32[1]{0:T(128)S(6)} %copy.23.cut_ref, f32[1024,8,128]{2,1,0:T(8,128)} %bitcast.27, f32[1024,8,128]{2,1,0:T(8,128)} %bitcast.28, bf16[256,256]{1,0:T(8,128)(2,1)S(1)} %fusion.21.shift_ref), custom_call_target="tpu_custom_call" | custom-call | tf_op jit(solution)/shard_map/filter/pallas_call | solution.py:233
  170.9 0.0 copy-start
  170.9 2.0 copy-done
  172.9 22.1 %rotate.1 = (f32[128,8192]{1,0:T(8,128)}, f32[128,8192]{1,0:T(8,128)}, f32[256,256]{1,0:T(8,128)}, f32[256,256]{1,0:T(8,128)}, f32[128,128]{1,0:T(8,128)}, /*index=5*/f32[128,128]{1,0:T(8,128)}) custom-call(f32[256,256]{1,0:T(8,128)} %maximum_bitcast_fusion.eig_ref, f32[32,32,8,128]{3,2,1,0:T(8,128)} %copy-done, f32[32,32,8,128]{3,2,1,0:T(8,128)} %get-tuple-element.14.appl_ref), custom_call_target="tpu_custom_call" | custom-call | tf_op jit(solution)/shard_map/rotate/pallas_call | solution.py:313
  195.0 0.0 copy-start.2
  195.0 0.0 copy-start.1
  195.0 1.2 compare_select_fusion.1
  196.2 0.1 reshape.157
  196.3 0.1 reduce_sum.54
  196.4 0.1 copy.19
  196.6 0.1 copy.20
  196.7 0.1 reshape.162
  196.7 0.1 reduce_sum.56
  196.9 0.1 copy.21
  197.0 0.1 copy.22
  197.1 0.0 copy-done.2
  197.1 0.1 reduce_sum.58
  197.2 0.0 copy-done.1
  197.2 0.1 reduce_sum.59
  197.4 0.1 pad.3.clone
  197.5 0.1 maximum_maximum_fusion.part_ref
  197.5 33.5 %reduce_parts.1 = f32[16,128]{1,0:T(8,128)S(1)} custom-call(f32[32,16,128]{2,1,0:T(8,128)S(1)} %maximum_maximum_fusion.part_ref), custom_call_target="tpu_custom_call" | custom-call | tf_op jit(solution)/shard_map/reduce_parts/pallas_call | solution.py:385
  231.1 0.0 copy-start.3
  231.1 6.1 %multiply_subtract_fusion = f32[128,8192]{1,0:T(8,128)} fusion(f32[128,8192]{1,0:T(8,128)} %get-tuple-element.20, f32[128,8192]{1,0:T(8,128)} %get-tuple-element.10, f32[128]{0:T(128)S(1)} %fusion.25), kind=kLoop, calls=%fused_computation | loop fusion | flops 2097152 | bytes 12583424 | tf_op jit(solution)/shard_map/sub | solution.py:429
  237.2 0.0 copy-done.3
  237.2 0.6 fusion.26
  (14 shorter events, 0.3 us)
Async XLA Ops:
  170.9 2.0 copy-start
  195.0 2.1 copy-start.2
  195.0 2.2 copy-start.1
  231.1 6.1 %copy-start.3 = (f32[128]{0:T(128)}, f32[128]{0:T(128)S(1)}, u32[]{:S(2)}) copy-start(f32[128]{0:T(128)S(1)} %fusion.25) | copy-start | bytes 1540
